TPU v7x, 32 devices: a whole 2x2x4 slice. The times are simulated.
32 devices in a mesh: grp: 16 (over z, x, core), blk: 2 (over y).
Axes of the slice: x: 2, y: 2, z: 4, core: 2. Of those that a mesh axis runs over, the one named last changes fastest.
Arguments:
- walker_matrix: float32 [16, 2, 1024, 1024], P('grp', 'blk'), may hold values from -6 to 6
- updates: bfloat16 [16, 2, 4, 1024, 256], P('grp', 'blk'), may hold values from -0.19921875 to 0.19921875
- update_rows: int32 [16, 2, 4, 256], P('grp', 'blk'), may hold values from 0 to 1023, as said below
- left_table: float32 [1024, 256], replicated, may hold values from -0.1875 to 0.1875
- right_table: float32 [1024, 256], replicated, may hold values from -0.1875 to 0.1875
- assignment: int32 [2, 16], P('blk'), may hold values from 0 to 15, each once within a row
- momentum_sum: int32 [16, 16], replicated, may hold values from 0 to 15, as said below
- transfer_momentum: int32 [8], replicated, may hold values from 0 to 15
- transfer_frequency: int32 [8], replicated, may hold values from 0 to 15
- ownership: int32 [8], P('blk'), may hold values from 0 to 7, each once
- g4_prior: float32 [16, 8, 256, 256], P('grp', 'blk'), may hold values from -6 to 6
Outputs:
- g4_slices: float32 [16, 8, 256, 256], P('grp', 'blk')
Inputs may be any that keep to these rules, and one draw needn't show every extreme that they name: `update_rows`: within each update of each walker the 256 row indices are distinct. `assignment`: each row is a permutation of the grp indices. `momentum_sum`: the addition table of a periodic 4 x 4 cluster under a relabeling of its momenta; every row and column is a permutation. `ownership`: a permutation of the transfer slots.
All inputs are finite; a program needn't handle non-finite values.
Results may differ from a plain program's by a relative error of at most 0.0003.
Values sent between devices are 32-bit elements; how exact they have to be, the bound alone decides.
A program may use at most 128 MiB of HBM per device.

v0:
```python
import jax
import jax.numpy as jnp
from jax import lax
from jax.sharding import PartitionSpec as P

UPD = 4
NW = 16
KW = 256


highest = lax.Precision.HIGHEST


def measure_walker(matrix, updates_here, rows_here, left_table, right_table):
    for number in range(UPD):
        picked = matrix[rows_here[number]]
        matrix = matrix + jnp.dot(
            updates_here[number].astype(jnp.float32), picked, precision=highest
        )
    partial_value = jnp.dot(matrix, right_table, precision=highest)
    return jnp.dot(left_table.T, partial_value, precision=highest)


def shift_rows(momentum_sum, moment_ids, freq_ids):
    labels = jnp.arange(KW, dtype=jnp.int32)
    momenta = labels // NW
    frequency = labels % NW
    return (
        momentum_sum[momenta[None, :], moment_ids[:, None]] * NW
        + (frequency[None, :] + freq_ids[:, None]) % NW
    )


def cycle_terms(greens_cycle, shifted):
    flipped = jnp.swapaxes(greens_cycle, 1, 2)

    def one_transfer(row_ids):
        picked = jnp.take(flipped, row_ids, axis=1)
        picked = jnp.take(picked, row_ids, axis=2)
        return jnp.sum(greens_cycle * picked, axis=0)

    return jax.vmap(one_transfer)(shifted)


def shards(
    walker_matrix,
    updates,
    update_rows,
    left_table,
    right_table,
    assignment,
    momentum_sum,
    transfer_momentum,
    transfer_frequency,
    ownership,
    g4_prior,
):
    greens = measure_walker(
        walker_matrix[0, 0], updates[0, 0], update_rows[0, 0], left_table, right_table
    )
    groups = lax.axis_size("grp")
    targets = assignment[0]
    extent = greens.shape[0]
    pieces = greens.reshape(groups, extent // groups, extent)
    spread = lax.all_to_all(pieces, "grp", split_axis=0, concat_axis=0, tiled=True)
    arranged = jnp.zeros_like(spread).at[targets].set(spread)
    returned = lax.all_to_all(arranged, "grp", split_axis=0, concat_axis=0, tiled=True)
    measured = returned.reshape(extent, extent)
    shifted = shift_rows(momentum_sum, transfer_momentum[ownership], transfer_frequency[ownership])
    summed = cycle_terms(lax.all_gather(measured[None], "blk", axis=0, tiled=True), shifted)
    return (g4_prior[0] + summed * (1.0 / lax.axis_size("blk")))[None]


def solution(mesh):
    placed = (
        P("grp", "blk", None, None),
        P("grp", "blk", None, None, None),
        P("grp", "blk", None, None),
        P(),
        P(),
        P("blk", None),
        P(),
        P(),
        P(),
        P("blk"),
        P("grp", "blk", None, None),
    )
    return jax.shard_map(
        shards, mesh=mesh, in_specs=placed, out_specs=P("grp", "blk", None, None), check_vma=False
    )
```

profile of v0, /device:TPU:0, one launch (start us, length us, event | category | flops | bytes accessed | tf_op | source)
XLA Modules:
  0.0 170.2 jit_solution(5582205900483753604)
XLA Ops:
  0.0 0.0 copy-start
  0.0 0.8 compare_select_fusion.2
  0.9 5.4 %copy.35 = f32[1,1,1024,1024]{2,3,1,0:T(8,128)} copy(f32[1,1,1024,1024]{3,2,1,0:T(8,128)} %param.11) | data formatting | bytes 8388608 | tf_op args[0]
  6.2 3.8 %gather_fusion = f32[256,1024]{1,0:T(8,128)S(1)} fusion(f32[1024,1024]{1,0:T(8,128)} %bitcast.75, s32[1024]{0:T(1024)S(1)} %pad_clamp_fusion.4), kind=kCustom, calls=%fused_computation | custom fusion | bytes 2098176 | tf_op jit(solution)/shard_map/gather | solution.py:16
  10.0 7.7 %bitcast_add_fusion.4 = f32[1024,1024]{0,1:T(8,128)} fusion(f32[1,1,1024,1024]{2,3,1,0:T(8,128)} %copy.35, f32[256,1024]{1,0:T(8,128)S(1)} %gather_fusion, bf16[1,1,4,1024,256]{4,3,2,1,0:T(8,128)(2,1)} %param.12), kind=kOutput, calls=%fused_computation.14 | convolution fusion | flops 3222274048 | bytes 9961472 | tf_op jit(solution)/shard_map/dot_general | solution.py:17
  17.7 5.4 %copy.37 = f32[1024,1024]{1,0:T(8,128)} copy(f32[1024,1024]{0,1:T(8,128)} %bitcast_add_fusion.4) | data formatting | bytes 8388608 | tf_op jit(solution)/shard_map/add | solution.py:17
  23.1 3.8 %gather_fusion.1 = f32[256,1024]{1,0:T(8,128)S(1)} fusion(f32[1024,1024]{1,0:T(8,128)} %copy.37, s32[1024]{0:T(1024)S(1)} %pad_clamp_fusion.3), kind=kCustom, calls=%fused_computation.1 | custom fusion | bytes 2098176 | tf_op jit(solution)/shard_map/gather | solution.py:16
  26.9 7.7 %bitcast_add_fusion.3 = f32[1024,1024]{0,1:T(8,128)} fusion(f32[1024,1024]{0,1:T(8,128)} %bitcast_add_fusion.4, f32[256,1024]{1,0:T(8,128)S(1)} %gather_fusion.1, bf16[1,1,4,1024,256]{4,3,2,1,0:T(8,128)(2,1)} %param.12), kind=kOutput, calls=%fused_computation.13 | convolution fusion | flops 3222274048 | bytes 9961472 | tf_op jit(solution)/shard_map/dot_general | solution.py:17
  34.6 17.0 %copy.38 = f32[1024,1024]{1,0:T(8,128)} copy(f32[1024,1024]{0,1:T(8,128)} %bitcast_add_fusion.3) | data formatting | bytes 8388608 | tf_op jit(solution)/shard_map/add | solution.py:17
  51.6 3.8 %gather_fusion.2 = f32[256,1024]{1,0:T(8,128)S(1)} fusion(f32[1024,1024]{1,0:T(8,128)} %copy.38, s32[1024]{0:T(1024)S(1)} %pad_clamp_fusion.2), kind=kCustom, calls=%fused_computation.2 | custom fusion | bytes 2098176 | tf_op jit(solution)/shard_map/gather | solution.py:16
  55.4 7.7 %bitcast_add_fusion.2 = f32[1024,1024]{0,1:T(8,128)} fusion(f32[1024,1024]{0,1:T(8,128)} %bitcast_add_fusion.3, f32[256,1024]{1,0:T(8,128)S(1)} %gather_fusion.2, bf16[1,1,4,1024,256]{4,3,2,1,0:T(8,128)(2,1)} %param.12), kind=kOutput, calls=%fused_computation.12 | convolution fusion | flops 3222274048 | bytes 9961472 | tf_op jit(solution)/shard_map/dot_general | solution.py:17
  63.1 5.4 %copy.39 = f32[1024,1024]{1,0:T(8,128)} copy(f32[1024,1024]{0,1:T(8,128)} %bitcast_add_fusion.2) | data formatting | bytes 8388608 | tf_op jit(solution)/shard_map/add | solution.py:17
  68.5 3.8 %gather_fusion.3 = f32[256,1024]{1,0:T(8,128)S(1)} fusion(f32[1024,1024]{1,0:T(8,128)} %copy.39, s32[1024]{0:T(1024)S(1)} %pad_clamp_fusion.1), kind=kCustom, calls=%fused_computation.3 | custom fusion | bytes 2098176 | tf_op jit(solution)/shard_map/gather | solution.py:16
  72.3 0.0 copy-start.4
  72.3 4.7 %fusion.2 = f32[1024,1024]{1,0:T(8,128)S(1)} fusion(f32[256,1024]{1,0:T(8,128)S(1)} %gather_fusion.3, bf16[1,1,4,1024,256]{4,3,2,1,0:T(8,128)(2,1)} %param.12), kind=kOutput, calls=%fused_computation.19 | convolution fusion | flops 3221225472 | bytes 5767168 | tf_op jit(solution)/shard_map/dot_general | solution.py:17
  77.0 0.0 copy-done
  77.0 0.0 copy-done.4
  77.1 0.0 copy-start.6
  77.1 0.0 copy-start.7
  77.1 0.0 copy-start.2
  77.1 6.8 %fusion = f32[1024,256]{1,0:T(8,128)S(1)} fusion(f32[1024,256]{1,0:T(8,128)S(1)} %copy-done, f32[1024,1024]{0,1:T(8,128)S(1)} %copy-done.4, f32[1024,1024]{1,0:T(8,128)S(1)} %fusion.2), kind=kOutput, calls=%fused_computation.11 | convolution fusion | flops 3222274048 | bytes 10485760 | tf_op jit(solution)/shard_map/dot_general | solution.py:20
  83.9 0.0 copy-start.1
  83.9 0.0 copy-start.3
  83.9 0.0 copy-start.8
  83.9 2.8 %fusion.22 = f32[256,256]{0,1:T(8,128)} fusion(f32[1024,256]{1,0:T(8,128)S(1)} %fusion, f32[1024,256]{1,0:T(8,128)S(1)} %copy-done.6), kind=kOutput, calls=%fused_computation.74 | convolution fusion | flops 805306368 | bytes 2359296 | tf_op jit(solution)/shard_map/dot_general | solution.py:21
  86.7 7.4 %all-to-all-start = ((f32[16,16,256]{2,1,0:T(8,128)}), f32[16,16,256]{2,1,0:T(8,128)S(1)}, u32[]{:S(2)}, u32[]{:S(2)}) async-start(f32[16,16,256]{2,1,0:T(8,128)} %bitcast.21), calls=%async_computation | async-start | bytes 524288 | tf_op jit(solution)/shard_map/all_to_all | solution.py:65
  94.1 0.6 gather_fusion.4
  94.8 0.1 or_bitcast_fusion.1
  94.9 7.1 %gather_fusion.5 = s32[1024]{0:T(1024)S(1)} fusion(s32[16,16]{1,0:T(8,128)S(1)} %copy-done.1, s32[1024]{0:T(1024)S(1)} %bitcast.74), kind=kCustom, calls=%fused_computation.5 | custom fusion | bytes 16384 | tf_op jit(solution)/shard_map/gather | solution.py:29
  102.0 0.6 gather_fusion.6
  102.6 1.5 all-to-all-done
  104.1 0.7 broadcast_in_dim.20
  104.8 2.5 %scatter_fusion = f32[16,16,256]{2,1,0:T(8,128)} fusion(f32[16,16,256]{2,1,0:T(8,128)} %broadcast_in_dim.20, s32[16]{0:T(128)S(1)} %fusion.19, f32[16,16,256]{2,1,0:T(8,128)S(1)} %all-to-all-done), kind=kCustom, calls=%fused_computation.9 | custom fusion | bytes 786496 | tf_op jit(solution)/shard_map/scatter | solution.py:66
  107.3 4.5 %all-to-all-start.1 = ((f32[16,16,256]{2,1,0:T(8,128)}), f32[16,16,256]{2,1,0:T(8,128)S(1)}, u32[]{:S(2)}, u32[]{:S(2)}) async-start(f32[16,16,256]{2,1,0:T(8,128)} %scatter_fusion), calls=%async_computation.1 | async-start | bytes 524288 | tf_op jit(solution)/shard_map/all_to_all | solution.py:67
  111.8 0.1 or_bitcast_fusion
  111.9 0.1 compare_and_fusion
  112.0 9.8 %all-to-all-done.1 = f32[16,16,256]{2,1,0:T(8,128)S(1)} async-done(((f32[16,16,256]{2,1,0:T(8,128)}), f32[16,16,256]{2,1,0:T(8,128)S(1)}, u32[]{:S(2)}, u32[]{:S(2)}) %all-to-all-start.1) | async-done | bytes 262176 | tf_op jit(solution)/shard_map/all_to_all | solution.py:67
  121.8 8.8 %all_gather.3 = f32[2,256,256]{2,1,0:T(8,128)S(1)} all-gather(f32[1,256,256]{2,1,0:T(8,128)S(1)} %bitcast.79), channel_id=1, replica_groups=mesh['grp'=16,'blk'=2] {'blk'}, dimensions={0}, use_global_device_ids=true | all-gather | bytes 786432 | tf_op jit(solution)/shard_map/all_gather | solution.py:70
  130.6 0.2 copy.41
  130.8 1.2 copy.40
  132.0 8.9 %gather_fusion.7 = f32[1024,2,256]{2,1,0:T(2,128)} fusion(f32[2,256,256]{2,0,1:T(2,128)S(1)} %bitcast.76, s32[1024]{0:T(1024)S(1)} %broadcast_clamp_fusion), kind=kCustom, calls=%fused_computation.7 | custom fusion | bytes 4198400 | tf_op jit(solution)/shard_map/vmap(jit(_take))/gather | solution.py:38
  140.9 6.0 %copy.42 = f32[4,256,2,256]{1,2,3,0:T(2,128)} copy(f32[4,256,2,256]{3,2,1,0:T(2,128)} %bitcast.77) | data formatting | bytes 4194304 | tf_op jit(solution)/shard_map/vmap(jit(_take))/gather | solution.py:38
  146.9 2.5 %select_bitcast_fusion = f32[4,2,256,256]{2,1,3,0:T(2,128)S(1)} fusion(f32[4,256,2,256]{1,2,3,0:T(2,128)} %copy.42, pred[4,256]{1,0:T(4,128)(4,1)S(1)} %compare_and_fusion), kind=kLoop, calls=%fused_computation.17 | loop fusion | flops 524288 | bytes 4195328 | tf_op jit(solution)/shard_map/vmap(jit(_take))/select_n | solution.py:38
  149.5 10.3 %gather_fusion.8 = f32[1024,2,256]{2,1,0:T(2,128)} fusion(f32[4,2,256,256]{2,1,3,0:T(2,128)S(1)} %select_bitcast_fusion, s32[1024]{0:T(1024)S(1)} %bitcast.73), kind=kCustom, calls=%fused_computation.8 | custom fusion | bytes 4202496 | tf_op jit(solution)/shard_map/vmap(jit(_take))/gather | solution.py:39
  159.8 4.6 %copy.43 = f32[4,256,2,256]{1,2,3,0:T(2,128)S(1)} copy(f32[4,256,2,256]{3,2,1,0:T(2,128)} %bitcast.78) | data formatting | bytes 4194304 | tf_op jit(solution)/shard_map/vmap(jit(_take))/gather | solution.py:39
  164.5 0.0 copy-start.5
  164.5 4.2 %fusion.1 = f32[4,256,256]{2,1,0:T(8,128)S(1)} fusion(f32[4,256,2,256]{1,2,3,0:T(2,128)S(1)} %copy.43, pred[4,256]{1,0:T(4,128)(4,1)S(1)} %compare_and_fusion, f32[2,256,256]{2,0,1:T(2,128)} %copy.40), kind=kLoop, calls=%fused_computation.16 | loop fusion | flops 1310720 | bytes 3671040 | tf_op jit(solution)/shard_map/vmap()/reduce_sum | solution.py:40
  168.7 1.1 bitcast_add_fusion.5
  (24 shorter events, 0.1 us)
Async XLA Ops:
  0.0 77.0 %copy-start = (f32[1024,256]{1,0:T(8,128)S(1)}, f32[1024,256]{1,0:T(8,128)}, u32[]{:S(2)}) copy-start(f32[1024,256]{1,0:T(8,128)} %param.15) | copy-start | bytes 3145732
  72.3 4.8 %copy-start.4 = (f32[1024,1024]{0,1:T(8,128)S(1)}, f32[1024,1024]{0,1:T(8,128)}, u32[]{:S(2)}) copy-start(f32[1024,1024]{0,1:T(8,128)} %bitcast_add_fusion.2) | copy-start | bytes 12582916
  77.1 6.8 %copy-start.6 = (f32[1024,256]{1,0:T(8,128)S(1)}, f32[1024,256]{1,0:T(8,128)}, u32[]{:S(2)}) copy-start(f32[1024,256]{1,0:T(8,128)} %param.14) | copy-start | bytes 3145732
  77.1 17.0 %copy-start.7 = (s32[4]{0:T(128)S(1)}, s32[4]{0:T(128)}, u32[]{:S(2)}) copy-start(s32[4]{0:T(128)} %param.20) | copy-start | bytes 52
  77.1 17.0 %copy-start.2 = (s32[8]{0:T(128)S(1)}, s32[8]{0:T(128)}, u32[]{:S(2)}) copy-start(s32[8]{0:T(128)} %param.18) | copy-start | bytes 100
  83.9 11.0 %copy-start.1 = (s32[16,16]{1,0:T(8,128)S(1)}, s32[16,16]{1,0:T(8,128)}, u32[]{:S(2)}) copy-start(s32[16,16]{1,0:T(8,128)} %param.17) | copy-start | bytes 3076
  83.9 18.1 %copy-start.3 = (s32[8]{0:T(128)S(1)}, s32[8]{0:T(128)}, u32[]{:S(2)}) copy-start(s32[8]{0:T(128)} %param.19) | copy-start | bytes 100
  83.9 18.7 %copy-start.8 = (s32[1,16]{1,0:T(1,128)S(1)}, s32[1,16]{1,0:T(1,128)}, u32[]{:S(2)}) copy-start(s32[1,16]{1,0:T(1,128)} %param.16) | copy-start | bytes 196
  86.7 17.4 %all-to-all-start = ((f32[16,16,256]{2,1,0:T(8,128)}), f32[16,16,256]{2,1,0:T(8,128)S(1)}, u32[]{:S(2)}, u32[]{:S(2)}) async-start(f32[16,16,256]{2,1,0:T(8,128)} %bitcast.21), calls=%async_computation | async-start | bytes 524288 | tf_op jit(solution)/shard_map/all_to_all | solution.py:65
  107.3 14.6 %all-to-all-start.1 = ((f32[16,16,256]{2,1,0:T(8,128)}), f32[16,16,256]{2,1,0:T(8,128)S(1)}, u32[]{:S(2)}, u32[]{:S(2)}) async-start(f32[16,16,256]{2,1,0:T(8,128)} %scatter_fusion), calls=%async_computation.1 | async-start | bytes 524288 | tf_op jit(solution)/shard_map/all_to_all | solution.py:67
  164.5 4.3 %copy-start.5 = (f32[1,4,256,256]{3,2,1,0:T(8,128)S(1)}, f32[1,4,256,256]{3,2,1,0:T(8,128)}, u32[]{:S(2)}) copy-start(f32[1,4,256,256]{3,2,1,0:T(8,128)} %param.21) | copy-start | bytes 3145732
where the time goes:
time: 173 us; the launch traced here: 170 us
  local copies, waits for them, and re-layouts  91 us (53%)
  matrix products  37.5 us (22%)
  starting transfers between devices  11.9 us (7%)
  waiting for transfers between devices  11.3 us (7%)
  other arithmetic  9.03 us (5%)
  blocking collectives  8.77 us (5%)
    dot_general x4, matrix products, measure_walker(): jnp.dot(updates_here[number].astype(jnp.float32), picked, precision=highest)  28 us
    add x3, local copies, waits for them, and re-layouts, measure_walker(): matrix + jnp.dot(updates_here[number].astype(jnp.float32), picked, precis...  27.7 us
    gather x4, local copies, waits for them, and re-layouts, measure_walker(): picked = matrix[rows_here[number]]  15 us
    gather x2, local copies, waits for them, and re-layouts, one_transfer(): picked = jnp.take(picked, row_ids, axis=2)  15 us
    gather x2, local copies, waits for them, and re-layouts, one_transfer(): picked = jnp.take(flipped, row_ids, axis=1)  14.9 us
    all_to_all x1, waiting for transfers between devices, shards(): lax.all_to_all(arranged, 'grp', split_axis=0, concat_axis=0, tiled=True)  9.8 us
    all_gather x1, blocking collectives, shards(): lax.all_gather(measured[None], 'blk', axis=0, tiled=True)  8.77 us
    all_to_all x1, starting transfers between devices, shards(): lax.all_to_all(pieces, 'grp', split_axis=0, concat_axis=0, tiled=True)  7.39 us
  transfers between devices with their start and end apart: 2, of which 2 were waited for; matrix products, arithmetic and copies ran while one was open for 5% of the time, Pallas kernels for 0%

commit v1 on v0

v1 whole, which is shorter than its diff:
```python
import functools

import jax
import jax.numpy as jnp
from jax import lax
from jax.experimental import pallas as pl
from jax.experimental.pallas import tpu as pltpu
from jax.sharding import PartitionSpec as P

MESH = pl.DeviceIdType.MESH
F32 = jnp.float32
BF16 = jnp.bfloat16


def split(x):
    hi = x.astype(BF16)
    return hi, (x - hi.astype(F32)).astype(BF16)


def nn(a, b):
    return jnp.dot(a, b, preferred_element_type=F32)


def nt(a, b):
    return lax.dot_general(a, b, (((1,), (1,)), ((), ())), preferred_element_type=F32)


def walker_kernel(m_hbm, u_hbm, rows_ref, l_hbm, r_hbm, out_ref, m_v, u_v, l_v, r_v, sems):
    number, order, rank = u_v.shape
    parts = 4
    step = order // parts
    copy_l = pltpu.make_async_copy(l_hbm, l_v, sems.at[0])
    copy_r = pltpu.make_async_copy(r_hbm, r_v, sems.at[1])
    copy_u = [pltpu.make_async_copy(u_hbm.at[i], u_v.at[i], sems.at[2 + i]) for i in range(number)]
    copy_m = [
        pltpu.make_async_copy(m_hbm.at[pl.ds(i * step, step)], m_v.at[pl.ds(i * step, step)], sems.at[2 + number + i])
        for i in range(parts)
    ]
    copy_l.start()
    for i in reversed(range(number)):
        copy_u[i].start()
    for c in copy_m:
        c.start()
    copy_r.start()
    copy_l.wait()
    w = jnp.transpose(l_v[...])
    for i in reversed(range(number)):
        pick = jnp.where(
            lax.broadcasted_iota(jnp.int32, (order, rank), 0) == rows_ref[pl.ds(i, 1), :], 1.0, 0.0
        ).astype(BF16)
        hi, lo = split(w)
        copy_u[i].wait()
        u = u_v[i]
        thi, tlo = split(nn(hi, u) + nn(lo, u))
        w = w + (nt(thi, pick) + nt(tlo, pick))
    hi, lo = split(w)
    v = None
    for i in range(parts):
        copy_m[i].wait()
        mh, ml = split(m_v[pl.ds(i * step, step), :])
        a, b = hi[:, i * step:(i + 1) * step], lo[:, i * step:(i + 1) * step]
        term = nn(a, mh) + nn(a, ml) + nn(b, mh)
        v = term if v is None else v + term
    vh, vl = split(v)
    copy_r.wait()
    rh, rl = split(r_v[...])
    out_ref[...] = nn(vh, rh) + nn(vh, rl) + nn(vl, rh)


def exchange_kernel(groups, blocks, target_ref, g_ref, out_ref, spread, arranged, s1, r1, s2, r2, s3, r3):
    grp = lax.axis_index("grp")
    blk = lax.axis_index("blk")

    def group_peer(i):
        return {"grp": lax.rem(grp + i, groups), "blk": blk}

    def block_peer(i):
        return {"grp": grp, "blk": lax.rem(blk + i, blocks)}

    barrier = pltpu.get_barrier_semaphore()

    @pl.loop(1, groups)
    def _(i):
        pl.semaphore_signal(barrier, inc=1, device_id=group_peer(i), device_id_type=MESH)

    @pl.loop(1, blocks)
    def _(i):
        pl.semaphore_signal(barrier, inc=1, device_id=block_peer(i), device_id_type=MESH)

    pl.semaphore_wait(barrier, groups + blocks - 2)

    def first(i):
        return pltpu.make_async_remote_copy(
            g_ref.at[lax.rem(grp + i, groups)], spread.at[grp], s1.at[i], r1.at[i],
            device_id=group_peer(i), device_id_type=MESH)

    def second(i):
        return pltpu.make_async_remote_copy(
            arranged.at[lax.rem(grp + i, groups)], out_ref.at[blk, grp], s2.at[i], r2.at[i],
            device_id=group_peer(i), device_id_type=MESH)

    def third(i, k):
        piece = out_ref.at[blk, lax.rem(grp + groups - i, groups)]
        return pltpu.make_async_remote_copy(
            piece, piece, s3.at[i, k], r3.at[i, k], device_id=block_peer(k), device_id_type=MESH)

    @pl.loop(1, groups)
    def _(i):
        first(i).start()

    spread[grp] = g_ref[grp]

    def source_of(a):
        return lax.fori_loop(0, groups, lambda w, s: jnp.where(target_ref[0, w] == a, w, s), 0)

    @pl.loop(1, groups)
    def _(i):
        first(i).wait_recv()

    @pl.loop(1, groups)
    def _(i):
        a = lax.rem(grp + i, groups)
        arranged[a] = spread[source_of(a)]
        second(i).start()

    out_ref[blk, grp] = spread[source_of(grp)]

    for k in range(1, blocks):
        third(0, k).start()

    @pl.loop(1, groups)
    def _(i):
        second(i).wait_recv()
        for k in range(1, blocks):
            third(i, k).start()

    @pl.loop(0, groups)
    def _(i):
        for k in range(1, blocks):
            third(i, k).wait_recv()

    @pl.loop(0, groups)
    def _(i):
        for k in range(1, blocks):
            third(i, k).wait_send()

    @pl.loop(1, groups)
    def _(i):
        first(i).wait_send()
        second(i).wait_send()


def cycle_kernel(own_ref, mom_ref, freq_ref, sum_ref, g_ref, prior_ref, out_ref, parts_v, perm_v):
    j = pl.program_id(0)
    blocks, kw, _ = g_ref.shape
    momenta = sum_ref.shape[0]
    nw = kw // momenta

    @pl.when(j == 0)
    def _():
        for b in range(blocks):
            hi, lo = split(g_ref[b])
            parts_v[b, :kw, :] = hi
            parts_v[b, kw:, :] = lo

    t = own_ref[j]
    q = mom_ref[t]
    f = freq_ref[t]
    lane = lax.broadcasted_iota(jnp.int32, (nw, kw), 1)
    nu = lax.rem(lax.broadcasted_iota(jnp.int32, (nw, kw), 0) + f, nw)
    base = lane - nu
    for kappa in range(momenta):
        hit = jnp.where(base == sum_ref[kappa, q] * nw, 1.0, 0.0).astype(BF16)
        perm_v[kappa * nw:(kappa + 1) * nw, :kw] = hit
        perm_v[kappa * nw:(kappa + 1) * nw, kw:] = hit
    both = perm_v[...]
    total = None
    for b in range(blocks):
        x = nt(both[:, :kw], parts_v[b]).astype(BF16)
        term = g_ref[b] * nt(x, both)
        total = term if total is None else total + term
    out_ref[0] = prior_ref[0] + total * (1.0 / blocks)


def shards(
    walker_matrix,
    updates,
    update_rows,
    left_table,
    right_table,
    assignment,
    momentum_sum,
    transfer_momentum,
    transfer_frequency,
    ownership,
    g4_prior,
):
    groups = lax.axis_size("grp")
    blocks = lax.axis_size("blk")
    order, kw = left_table.shape
    number, rank = updates.shape[2], updates.shape[4]
    anyspace = pl.BlockSpec(memory_space=pl.ANY)
    vmem = pl.BlockSpec(memory_space=pltpu.VMEM)
    smem = pl.BlockSpec(memory_space=pltpu.SMEM)
    greens = pl.pallas_call(
        walker_kernel,
        out_shape=jax.ShapeDtypeStruct((kw, kw), F32),
        in_specs=[anyspace, anyspace, vmem, anyspace, anyspace],
        out_specs=vmem,
        scratch_shapes=[
            pltpu.VMEM((order, order), F32),
            pltpu.VMEM((number, order, rank), BF16),
            pltpu.VMEM((order, kw), F32),
            pltpu.VMEM((order, kw), F32),
            pltpu.SemaphoreType.DMA((number + 6,)),
        ],
        compiler_params=pltpu.CompilerParams(vmem_limit_bytes=48 * 2**20),
        name="walker",
    )(walker_matrix[0, 0], updates[0, 0], update_rows[0, 0], left_table, right_table)

    rows = kw // groups
    measured = pl.pallas_call(
        functools.partial(exchange_kernel, groups, blocks),
        out_shape=jax.ShapeDtypeStruct((blocks, groups, rows, kw), F32),
        in_specs=[smem, vmem],
        out_specs=vmem,
        scratch_shapes=[
            pltpu.VMEM((groups, rows, kw), F32),
            pltpu.VMEM((groups, rows, kw), F32),
            pltpu.SemaphoreType.DMA((groups,)),
            pltpu.SemaphoreType.DMA((groups,)),
            pltpu.SemaphoreType.DMA((groups,)),
            pltpu.SemaphoreType.DMA((groups,)),
            pltpu.SemaphoreType.DMA((groups, blocks)),
            pltpu.SemaphoreType.DMA((groups, blocks)),
        ],
        compiler_params=pltpu.CompilerParams(
            collective_id=0, has_side_effects=True, vmem_limit_bytes=16 * 2**20),
        name="exchange",
    )(assignment, greens.reshape(groups, rows, kw)).reshape(blocks, kw, kw)

    slots = g4_prior.shape[1]
    whole = pl.BlockSpec((blocks, kw, kw), lambda j, *_: (0, 0, 0))
    block = pl.BlockSpec((1, kw, kw), lambda j, *_: (j, 0, 0))
    out = pl.pallas_call(
        cycle_kernel,
        out_shape=jax.ShapeDtypeStruct((slots, kw, kw), F32),
        grid_spec=pltpu.PrefetchScalarGridSpec(
            num_scalar_prefetch=4,
            grid=(slots,),
            in_specs=[whole, block],
            out_specs=block,
            scratch_shapes=[
                pltpu.VMEM((blocks, 2 * kw, kw), BF16),
                pltpu.VMEM((kw, 2 * kw), BF16),
            ],
        ),
        compiler_params=pltpu.CompilerParams(vmem_limit_bytes=24 * 2**20),
        name="cycle",
    )(ownership, transfer_momentum, transfer_frequency, momentum_sum, measured, g4_prior[0])
    return out[None]


def solution(mesh):
    placed = (
        P("grp", "blk", None, None),
        P("grp", "blk", None, None, None),
        P("grp", "blk", None, None),
        P(),
        P(),
        P("blk", None),
        P(),
        P(),
        P(),
        P("blk"),
        P("grp", "blk", None, None),
    )
    return jax.shard_map(
        shards, mesh=mesh, in_specs=placed, out_specs=P("grp", "blk", None, None), check_vma=False
    )
```

time: 173 us -> 45.8 us (0.26); the launches traced: 170 us -> 45.5 us
  local copies, waits for them, and re-layouts: 91 us -> 4.75 us
  Pallas kernels: 0 us -> 40.7 us
  matrix products: 37.5 us -> 0 us
  starting transfers between devices: 11.9 us -> 0 us
  waiting for transfers between devices: 11.3 us -> 0 us
  other arithmetic: 9.03 us -> 0 us
  blocking collectives: 8.77 us -> 0 us
    gather x11 -> x0, local copies, waits for them, and re-layouts: 53.2 us -> none  [the longest x4 15 us: measure_walker(): picked = matrix[rows_here[number]]]
    pallas_call x0 -> x3, Pallas kernels: none -> 40.7 us  [the longest x1 27.6 us: shards(): pl.pallas_call(functools.partial(exchange_kernel, groups, blocks), out_sh...]
    dot_general x6 -> x0, matrix products: 37.5 us -> none  [the longest x4 28 us: measure_walker(): jnp.dot(updates_here[number].astype(jnp.float32), picked, precision=highest)]
    add x3 -> x0, local copies, waits for them, and re-layouts: 27.7 us -> none  [measure_walker(): matrix + jnp.dot(updates_here[number].astype(jnp.float32), picked, precis...]
    all_to_all x2 -> x0, starting transfers between devices: 11.9 us -> none  [the longest x1 7.39 us: shards(): lax.all_to_all(pieces, 'grp', split_axis=0, concat_axis=0, tiled=True)]
    all_to_all x2 -> x0, waiting for transfers between devices: 11.3 us -> none  [the longest x1 9.8 us: shards(): lax.all_to_all(arranged, 'grp', split_axis=0, concat_axis=0, tiled=True)]
    all_gather x1 -> x0, blocking collectives: 8.77 us -> none  [shards(): lax.all_gather(measured[None], 'blk', axis=0, tiled=True)]
    reduce_sum x1 -> x0, other arithmetic: 4.24 us -> none  [one_transfer(): return jnp.sum(greens_cycle * picked, axis=0)]
  transfers between devices with their start and end apart: 2 -> 0, of which waited for: 2 -> 0; matrix products, arithmetic and copies ran while one was open for 5% -> 0% of each run, Pallas kernels for 0% -> 0%
where the time goes in v1:
time: 45.8 us; the launch traced here: 45.5 us
  Pallas kernels  40.7 us (89%)
  local copies, waits for them, and re-layouts  4.75 us (10%)
    pallas_call x1, Pallas kernels, shards(): pl.pallas_call(functools.partial(exchange_kernel, groups, blocks), out_sh...  27.6 us
    pallas_call x1, Pallas kernels, shards(): pl.pallas_call(walker_kernel, out_shape=jax.ShapeDtypeStruct((kw, kw), F3...  9.17 us
    unnamed x20, local copies, waits for them, and re-layouts  4.75 us
    pallas_call x1, Pallas kernels, shards(): pl.pallas_call(cycle_kernel, out_shape=jax.ShapeDtypeStruct((slots, kw, k...  3.96 us

profile of v1, /device:TPU:0, one launch (start us, length us, event | category | flops | bytes accessed | tf_op | source)
XLA Modules:
  0.0 45.5 jit_solution(9571050745214801529)
XLA Ops:
  0.0 0.0 copy-start
  0.0 1.6 %copy-done = bf16[1,1,4,1024,256]{4,3,2,1,0:T(8,128)(2,1)S(1)} copy-done((bf16[1,1,4,1024,256]{4,3,2,1,0:T(8,128)(2,1)S(1)}, bf16[1,1,4,1024,256]{4,3,2,1,0:T(8,128)(2,1)}, u32[]{:S(2)}) %copy-start) | copy-done | bytes 2097176
  1.6 0.0 copy-start.2
  1.6 1.2 %copy-done.2 = f32[1024,256]{1,0:T(8,128)S(1)} copy-done((f32[1024,256]{1,0:T(8,128)S(1)}, f32[1024,256]{1,0:T(8,128)}, u32[]{:S(2)}) %copy-start.2) | copy-done | bytes 1048600
  2.8 0.0 copy-start.3
  2.8 1.2 %copy-done.3 = f32[1024,256]{1,0:T(8,128)S(1)} copy-done((f32[1024,256]{1,0:T(8,128)S(1)}, f32[1024,256]{1,0:T(8,128)}, u32[]{:S(2)}) %copy-start.3) | copy-done | bytes 1048600
  4.0 0.0 copy-start.5
  4.0 0.7 %copy-done.5 = s32[1,1,4,256]{3,2,1,0:T(4,128)S(1)} copy-done((s32[1,1,4,256]{3,2,1,0:T(4,128)S(1)}, s32[1,1,4,256]{3,2,1,0:T(4,128)}, u32[]{:S(2)}) %copy-start.5) | copy-done | bytes 4120
  4.7 0.0 copy-start.6
  4.7 0.0 copy-start.1
  4.7 0.0 copy-start.4
  4.7 0.0 copy-start.7
  4.7 0.0 copy-start.8
  4.8 0.0 copy-start.9
  4.8 9.2 %walker.1 = f32[256,256]{1,0:T(8,128)S(1)} custom-call(f32[1024,1024]{1,0:T(8,128)} %bitcast.12, bf16[4,1024,256]{2,1,0:T(8,128)(2,1)S(1)} %bitcast.8, s32[4,256]{1,0:T(4,128)S(1)} %bitcast.11, f32[1024,256]{1,0:T(8,128)S(1)} %copy-done.2, f32[1024,256]{1,0:T(8,128)S(1)} %copy-done.3), custom_call_target="tpu_custom_call" | custom-call | tf_op jit(solution)/shard_map/walker/pallas_call | solution.py:205
  13.9 0.0 copy-done.6
  13.9 27.6 %exchange.1 = f32[2,16,16,256]{3,2,1,0:T(8,128)S(1)} custom-call(s32[1,16]{1,0:T(1,128)S(1)} %copy-done.6, f32[16,16,256]{2,1,0:T(8,128)S(1)} %bitcast.10), custom_call_target="tpu_custom_call" | custom-call | tf_op jit(solution)/shard_map/exchange/pallas_call | solution.py:222
  41.5 0.0 copy-done.1
  41.5 0.0 copy-done.4
  41.5 0.0 copy-done.7
  41.6 0.0 copy-done.8
  41.6 0.0 copy-done.9
  41.6 4.0 %cycle.1 = f32[4,256,256]{2,1,0:T(8,128)} custom-call(s32[4]{0:T(128)S(1)} %copy-done.7, s32[8]{0:T(128)S(1)} %copy-done.8, s32[8]{0:T(128)S(1)} %copy-done.9, s32[16,16]{1,0:T(8,128)S(1)} %copy-done.4, f32[2,256,256]{2,1,0:T(8,128)S(1)} %bitcast.7, f32[4,256,256]{2,1,0:T(8,128)S(1)} %bitcast.9), custom_call_target="tpu_custom_call" | custom-call | tf_op jit(solution)/shard_map/cycle/pallas_call | solution.py:245
Async XLA Ops:
  0.0 1.6 %copy-start = (bf16[1,1,4,1024,256]{4,3,2,1,0:T(8,128)(2,1)S(1)}, bf16[1,1,4,1024,256]{4,3,2,1,0:T(8,128)(2,1)}, u32[]{:S(2)}) copy-start(bf16[1,1,4,1024,256]{4,3,2,1,0:T(8,128)(2,1)} %param.12) | copy-start | bytes 6291460
  1.6 1.2 %copy-start.2 = (f32[1024,256]{1,0:T(8,128)S(1)}, f32[1024,256]{1,0:T(8,128)}, u32[]{:S(2)}) copy-start(f32[1024,256]{1,0:T(8,128)} %l_hbm.1) | copy-start | bytes 3145732
  2.8 1.2 %copy-start.3 = (f32[1024,256]{1,0:T(8,128)S(1)}, f32[1024,256]{1,0:T(8,128)}, u32[]{:S(2)}) copy-start(f32[1024,256]{1,0:T(8,128)} %r_hbm.1) | copy-start | bytes 3145732
  4.0 0.7 %copy-start.5 = (s32[1,1,4,256]{3,2,1,0:T(4,128)S(1)}, s32[1,1,4,256]{3,2,1,0:T(4,128)}, u32[]{:S(2)}) copy-start(s32[1,1,4,256]{3,2,1,0:T(4,128)} %param.13) | copy-start | bytes 12292
  4.7 9.2 %copy-start.6 = (s32[1,16]{1,0:T(1,128)S(1)}, s32[1,16]{1,0:T(1,128)}, u32[]{:S(2)}) copy-start(s32[1,16]{1,0:T(1,128)} %target_ref.1) | copy-start | bytes 196
  4.7 36.8 %copy-start.1 = (f32[1,4,256,256]{3,2,1,0:T(8,128)S(1)}, f32[1,4,256,256]{3,2,1,0:T(8,128)}, u32[]{:S(2)}) copy-start(f32[1,4,256,256]{3,2,1,0:T(8,128)} %param.21) | copy-start | bytes 3145732
  4.7 36.8 %copy-start.4 = (s32[16,16]{1,0:T(8,128)S(1)}, s32[16,16]{1,0:T(8,128)}, u32[]{:S(2)}) copy-start(s32[16,16]{1,0:T(8,128)} %sum_ref.1) | copy-start | bytes 3076
  4.7 36.8 %copy-start.7 = (s32[4]{0:T(128)S(1)}, s32[4]{0:T(128)}, u32[]{:S(2)}) copy-start(s32[4]{0:T(128)} %own_ref.1) | copy-start | bytes 52
  4.7 36.8 %copy-start.8 = (s32[8]{0:T(128)S(1)}, s32[8]{0:T(128)}, u32[]{:S(2)}) copy-start(s32[8]{0:T(128)} %mom_ref.1) | copy-start | bytes 100
  4.8 36.8 %copy-start.9 = (s32[8]{0:T(128)S(1)}, s32[8]{0:T(128)}, u32[]{:S(2)}) copy-start(s32[8]{0:T(128)} %freq_ref.1) | copy-start | bytes 100

commit v2 on v0

v2 whole, which is shorter than its diff:
```python
import functools

import jax
import jax.numpy as jnp
from jax import lax
from jax.experimental import pallas as pl
from jax.experimental.pallas import tpu as pltpu
from jax.sharding import PartitionSpec as P

MESH = pl.DeviceIdType.MESH
F32 = jnp.float32
BF16 = jnp.bfloat16


def split(x):
    hi = x.astype(BF16)
    return hi, (x - hi.astype(F32)).astype(BF16)


def nn(a, b):
    return jnp.dot(a, b, preferred_element_type=F32)


def nt(a, b):
    return lax.dot_general(a, b, (((1,), (1,)), ((), ())), preferred_element_type=F32)


def exchange_kernel(
    groups, blocks, target_ref, own_ref, mom_ref, freq_ref, sum_ref, m_hbm, u_hbm, rows_hbm, l_hbm, r_hbm, out_hbm,
    m_v, u_v, rows_v, l_v, r_v, pick_v, zh_v, zl_v, g_v, arranged, out_ref, perm_v, total_v, source,
    sems, out_sems, s1, r1, s2, r2, s3, r3, *spread,
):
    grp = lax.axis_index("grp")
    blk = lax.axis_index("blk")
    number, order, rank = u_v.shape
    halves, _, rows, kw = g_v.shape
    kh = kw // halves
    parts = 4
    step = order // parts

    def group_peer(i):
        return {"grp": lax.rem(grp + i, groups), "blk": blk}

    def block_peer(i):
        return {"grp": grp, "blk": lax.rem(blk + i, blocks)}

    copy_rows = pltpu.make_async_copy(rows_hbm, rows_v, sems.at[0])
    copy_l = pltpu.make_async_copy(l_hbm, l_v, sems.at[1])
    copy_r = pltpu.make_async_copy(r_hbm, r_v, sems.at[2])
    copy_u = [pltpu.make_async_copy(u_hbm.at[i], u_v.at[i], sems.at[3 + i]) for i in range(number)]
    copy_m = [
        pltpu.make_async_copy(m_hbm.at[pl.ds(i * step, step)], m_v.at[pl.ds(i * step, step)], sems.at[3 + number + i])
        for i in range(parts)
    ]
    copy_rows.start()
    copy_l.start()
    for i in reversed(range(number)):
        copy_u[i].start()
    copy_r.start()
    for c in copy_m:
        c.start()

    barrier = pltpu.get_barrier_semaphore()

    @pl.loop(1, groups)
    def _(i):
        pl.semaphore_signal(barrier, inc=1, device_id=group_peer(i), device_id_type=MESH)

    @pl.loop(1, blocks)
    def _(i):
        pl.semaphore_signal(barrier, inc=1, device_id=block_peer(i), device_id_type=MESH)

    targets = [target_ref[0, w] for w in range(groups)]
    for a in range(groups):
        found = 0
        for w in range(groups):
            found = jnp.where(targets[w] == a, w, found)
        source[a] = found

    copy_rows.wait()
    for i in reversed(range(number)):
        pick_v[i] = jnp.where(
            lax.broadcasted_iota(jnp.int32, (order, rank), 0) == rows_v[pl.ds(i, 1), :], 1.0, 0.0
        ).astype(BF16)

    slots = total_v.shape[0]
    momenta = sum_ref.shape[0]
    nw = kw // momenta
    sub = lax.broadcasted_iota(jnp.int32, (nw, kw), 0)
    lane = lax.broadcasted_iota(jnp.int32, (nw, kw), 1)
    for j in range(slots):
        t = own_ref[j]
        q = mom_ref[t]
        moved = sub + freq_ref[t]
        base = lane - jnp.where(moved >= nw, moved - nw, moved)
        for kappa in range(momenta):
            hit = jnp.where(base == sum_ref[kappa, q] * nw, 1.0, 0.0).astype(BF16)
            perm_v[j * kw + kappa * nw:j * kw + (kappa + 1) * nw, :] = hit

    def accumulate(b, fresh, last):
        g = out_ref[b].reshape(kw, kw)
        gh, gl = split(g)
        xh = nt(perm_v[...], gh).astype(BF16)
        xl = nt(perm_v[...], gl).astype(BF16)
        for j in range(slots):
            rows_j = slice(j * kw, (j + 1) * kw)
            y = nt(jnp.concatenate([xh[rows_j], xl[rows_j]], axis=0), perm_v[rows_j, :])
            term = g * (y[:kw] + y[kw:])
            total_v[j] = term if fresh else total_v[j] + term
            if last:
                pltpu.make_async_copy(total_v.at[j], out_hbm.at[j], out_sems.at[j]).start()

    def chain(h):
        w = jnp.transpose(l_v[:, h * kh:(h + 1) * kh])
        for i in reversed(range(number)):
            if h == 0:
                copy_u[i].wait()
            t = nn(jnp.concatenate(split(w), axis=0), u_v[i])
            t = nt(jnp.concatenate(split(t[:kh] + t[kh:]), axis=0), pick_v[i])
            w = w + (t[:kh] + t[kh:])
        return split(w)

    def finish(h, wh, wl):
        t = nn(jnp.concatenate([wh, wl], axis=0), zh_v[...])
        g = t[:kh] + t[kh:] + nn(wh, zl_v[...])
        g_v[h] = g.reshape(groups, rows, kw)

    def first(h, i):
        return pltpu.make_async_remote_copy(
            g_v.at[h, lax.rem(grp + i, groups)], spread[h].at[grp], s1.at[h, i], r1.at[h, i],
            device_id=group_peer(i), device_id_type=MESH)

    def second(h, i):
        return pltpu.make_async_remote_copy(
            arranged.at[h, lax.rem(grp + i, groups)], out_ref.at[blk, h, grp], s2.at[h, i], r2.at[h, i],
            device_id=group_peer(i), device_id_type=MESH)

    def third(h, i, k):
        piece = out_ref.at[blk, h, lax.rem(grp + groups - i, groups)]
        return pltpu.make_async_remote_copy(
            piece, piece, s3.at[h, i, k], r3.at[h, i, k], device_id=block_peer(k), device_id_type=MESH)

    copy_l.wait()
    wh, wl = chain(0)
    copy_r.wait()
    rh, rl = split(r_v[...])
    for i in range(parts):
        copy_m[i].wait()
        mh, ml = split(m_v[pl.ds(i * step, step), :])
        t = nn(jnp.concatenate([mh, ml], axis=0), rh)
        zh, zl = split(t[:step] + t[step:] + nn(mh, rl))
        zh_v[pl.ds(i * step, step), :] = zh
        zl_v[pl.ds(i * step, step), :] = zl
    finish(0, wh, wl)

    pl.semaphore_wait(barrier, groups + blocks - 2)

    for h in range(halves):
        if h > 0:
            finish(h, *chain(h))

        @pl.loop(1, groups)
        def _(i):
            first(h, i).start()

        spread[h][grp] = g_v[h, grp]

    for h in range(halves):
        @pl.loop(1, groups)
        def _(i):
            first(h, i).wait_recv()

        @pl.loop(1, groups)
        def _(i):
            a = lax.rem(grp + i, groups)
            arranged[h, a] = spread[h][source[a]]
            second(h, i).start()

        out_ref[blk, h, grp] = spread[h][source[grp]]
        for k in range(1, blocks):
            third(h, 0, k).start()

    for h in range(halves):
        @pl.loop(1, groups)
        def _(i):
            second(h, i).wait_recv()
            for k in range(1, blocks):
                third(h, i, k).start()

    accumulate(blk, True, blocks == 1)

    for k in range(1, blocks):
        for h in range(halves):
            @pl.loop(0, groups)
            def _(i):
                third(h, i, k).wait_recv()

        accumulate(lax.rem(blk + blocks - k, blocks), False, k == blocks - 1)

    for h in range(halves):
        @pl.loop(0, groups)
        def _(i):
            for k in range(1, blocks):
                third(h, i, k).wait_send()

        @pl.loop(1, groups)
        def _(i):
            first(h, i).wait_send()
            second(h, i).wait_send()

    for j in range(slots):
        pltpu.make_async_copy(total_v.at[j], out_hbm.at[j], out_sems.at[j]).wait()


def shards(
    walker_matrix,
    updates,
    update_rows,
    left_table,
    right_table,
    assignment,
    momentum_sum,
    transfer_momentum,
    transfer_frequency,
    ownership,
    g4_prior,
):
    groups = lax.axis_size("grp")
    blocks = lax.axis_size("blk")
    order, kw = left_table.shape
    number, rank = updates.shape[2], updates.shape[4]
    smem = pl.BlockSpec(memory_space=pltpu.SMEM)
    hbm = pl.BlockSpec(memory_space=pltpu.HBM)
    halves = 2 if kw // groups % 16 == 0 else 1
    rows = kw // groups // halves
    slots = g4_prior.shape[1]
    summed = pl.pallas_call(
        functools.partial(exchange_kernel, groups, blocks),
        out_shape=jax.ShapeDtypeStruct((slots, kw, kw), F32),
        in_specs=[smem] * 5 + [hbm] * 5,
        out_specs=hbm,
        scratch_shapes=[
            pltpu.VMEM((order, order), F32),
            pltpu.VMEM((number, order, rank), BF16),
            pltpu.VMEM((number, rank), jnp.int32),
            pltpu.VMEM((order, kw), F32),
            pltpu.VMEM((order, kw), F32),
            pltpu.VMEM((number, order, rank), BF16),
            pltpu.VMEM((order, kw), BF16),
            pltpu.VMEM((order, kw), BF16),
            pltpu.VMEM((halves, groups, rows, kw), F32),
            pltpu.VMEM((halves, groups, rows, kw), F32),
            pltpu.VMEM((blocks, halves, groups, rows, kw), F32),
            pltpu.VMEM((slots * kw, kw), BF16),
            pltpu.VMEM((slots, kw, kw), F32),
            pltpu.SMEM((groups,), jnp.int32),
            pltpu.SemaphoreType.DMA((number + 7,)),
            pltpu.SemaphoreType.DMA((slots,)),
            pltpu.SemaphoreType.DMA((halves, groups)),
            pltpu.SemaphoreType.DMA((halves, groups)),
            pltpu.SemaphoreType.DMA((halves, groups)),
            pltpu.SemaphoreType.DMA((halves, groups)),
            pltpu.SemaphoreType.DMA((halves, groups, blocks)),
            pltpu.SemaphoreType.DMA((halves, groups, blocks)),
        ] + [pltpu.VMEM((groups, rows, kw), F32)] * halves,
        compiler_params=pltpu.CompilerParams(
            collective_id=0, has_side_effects=True, vmem_limit_bytes=63 * 2**20 + 2**19),
        name="exchange",
    )(assignment, ownership, transfer_momentum, transfer_frequency, momentum_sum,
      walker_matrix[0, 0], updates[0, 0], update_rows[0, 0], left_table, right_table)
    return (g4_prior[0] + summed * (1.0 / blocks))[None]


def solution(mesh):
    placed = (
        P("grp", "blk", None, None),
        P("grp", "blk", None, None, None),
        P("grp", "blk", None, None),
        P(),
        P(),
        P("blk", None),
        P(),
        P(),
        P(),
        P("blk"),
        P("grp", "blk", None, None),
    )
    return jax.shard_map(
        shards, mesh=mesh, in_specs=placed, out_specs=P("grp", "blk", None, None), check_vma=False
    )
```

time: 173 us -> 37.7 us (0.22); the launches traced: 170 us -> 37.5 us
  local copies, waits for them, and re-layouts: 91 us -> 0 us
  matrix products: 37.5 us -> 0 us
  Pallas kernels: 0 us -> 34.8 us
  starting transfers between devices: 11.9 us -> 0 us
  waiting for transfers between devices: 11.3 us -> 0 us
  blocking collectives: 8.77 us -> 0 us
  other arithmetic: 9.03 us -> 2.65 us
    gather x11 -> x0, local copies, waits for them, and re-layouts: 53.2 us -> none  [the longest x4 15 us: measure_walker(): picked = matrix[rows_here[number]]]
    dot_general x6 -> x0, matrix products: 37.5 us -> none  [the longest x4 28 us: measure_walker(): jnp.dot(updates_here[number].astype(jnp.float32), picked, precision=highest)]
    pallas_call x0 -> x1, Pallas kernels: none -> 34.8 us  [shards(): pl.pallas_call(functools.partial(exchange_kernel, groups, blocks), out_sh...]
    add x3 -> x0, local copies, waits for them, and re-layouts: 27.7 us -> none  [measure_walker(): matrix + jnp.dot(updates_here[number].astype(jnp.float32), picked, precis...]
    all_to_all x2 -> x0, starting transfers between devices: 11.9 us -> none  [the longest x1 7.39 us: shards(): lax.all_to_all(pieces, 'grp', split_axis=0, concat_axis=0, tiled=True)]
    all_to_all x2 -> x0, waiting for transfers between devices: 11.3 us -> none  [the longest x1 9.8 us: shards(): lax.all_to_all(arranged, 'grp', split_axis=0, concat_axis=0, tiled=True)]
    all_gather x1 -> x0, blocking collectives: 8.77 us -> none  [shards(): lax.all_gather(measured[None], 'blk', axis=0, tiled=True)]
    unnamed x22 -> x0, local copies, waits for them, and re-layouts: 5.43 us -> none
  transfers between devices with their start and end apart: 2 -> 0, of which waited for: 2 -> 0; matrix products, arithmetic and copies ran while one was open for 5% -> 0% of each run, Pallas kernels for 0% -> 0%
where the time goes in v2:
time: 37.7 us; the launch traced here: 37.5 us
  Pallas kernels  34.8 us (92%)
  other arithmetic  2.65 us (7%)
    pallas_call x1, Pallas kernels, shards(): pl.pallas_call(functools.partial(exchange_kernel, groups, blocks), out_sh...  34.8 us
    broadcast_in_dim x1, other arithmetic, shards(): return (g4_prior[0] + summed * (1.0 / blocks))[None]  2.65 us

profile of v2, /device:TPU:0, one launch (start us, length us, event | category | flops | bytes accessed | tf_op | source)
XLA Modules:
  0.0 37.5 jit_solution(14272351087863960115)
XLA Ops:
  0.0 34.8 %exchange.1 = f32[4,256,256]{2,1,0:T(8,128)} custom-call(s32[1,16]{1,0:T(1,128)} %target_ref.1, s32[4]{0:T(128)} %own_ref.1, s32[8]{0:T(128)} %mom_ref.1, s32[8]{0:T(128)} %freq_ref.1, s32[16,16]{1,0:T(8,128)} %sum_ref.1, f32[1024,1024]{1,0:T(8,128)} %bitcast.9, bf16[4,1024,256]{2,1,0:T(8,128)(2,1)} %bitcast.10, s32[4,256]{1,0:T(4,128)} %bitcast.11, ...), custom_call_target="tpu_custom_call" | custom-call | tf_op jit(solution)/shard_map/exchange/pallas_call | solution.py:237
  34.8 2.6 %fusion = f32[1,4,256,256]{3,2,1,0:T(8,128)} fusion(f32[1,4,256,256]{3,2,1,0:T(8,128)} %param.21, f32[4,256,256]{2,1,0:T(8,128)} %exchange.1), kind=kLoop, calls=%fused_computation.1 | loop fusion | flops 524288 | bytes 3145728 | tf_op jit(solution)/shard_map/broadcast_in_dim | solution.py:271

commit v3 on v2

--- a/solution.py
+++ b/solution.py
@@ -25,8 +25,12 @@
     return lax.dot_general(a, b, (((1,), (1,)), ((), ())), preferred_element_type=F32)
 
 
+def partner_order(groups):
+    return list(range(1, groups))
+
+
 def exchange_kernel(
-    groups, blocks, target_ref, own_ref, mom_ref, freq_ref, sum_ref, m_hbm, u_hbm, rows_hbm, l_hbm, r_hbm, out_hbm,
+    groups, blocks, target_ref, own_ref, mom_ref, freq_ref, sum_ref, m_hbm, u_hbm, rows_hbm, l_hbm, r_hbm, prior_hbm, out_hbm,
     m_v, u_v, rows_v, l_v, r_v, pick_v, zh_v, zl_v, g_v, arranged, out_ref, perm_v, total_v, source,
     sems, out_sems, s1, r1, s2, r2, s3, r3, *spread,
 ):
@@ -38,8 +42,18 @@
     parts = 4
     step = order // parts
 
+    pairs = partner_order(groups)
+
+    def partner(i):
+        place, bit = grp, 1
+        while bit <= i:
+            if i & bit:
+                place = place + bit - 2 * bit * lax.rem(grp // bit, 2)
+            bit *= 2
+        return place
+
     def group_peer(i):
-        return {"grp": lax.rem(grp + i, groups), "blk": blk}
+        return {"grp": partner(i), "blk": blk}
 
     def block_peer(i):
         return {"grp": grp, "blk": lax.rem(blk + i, blocks)}
@@ -59,11 +73,12 @@
     copy_r.start()
     for c in copy_m:
         c.start()
+    copy_p = pltpu.make_async_copy(prior_hbm, total_v, sems.at[3 + number + parts])
+    copy_p.start()
 
     barrier = pltpu.get_barrier_semaphore()
 
-    @pl.loop(1, groups)
-    def _(i):
+    for i in pairs:
         pl.semaphore_signal(barrier, inc=1, device_id=group_peer(i), device_id_type=MESH)
 
     @pl.loop(1, blocks)
@@ -97,7 +112,7 @@
             hit = jnp.where(base == sum_ref[kappa, q] * nw, 1.0, 0.0).astype(BF16)
             perm_v[j * kw + kappa * nw:j * kw + (kappa + 1) * nw, :] = hit
 
-    def accumulate(b, fresh, last):
+    def accumulate(b, last):
         g = out_ref[b].reshape(kw, kw)
         gh, gl = split(g)
         xh = nt(perm_v[...], gh).astype(BF16)
@@ -106,7 +121,8 @@
             rows_j = slice(j * kw, (j + 1) * kw)
             y = nt(jnp.concatenate([xh[rows_j], xl[rows_j]], axis=0), perm_v[rows_j, :])
             term = g * (y[:kw] + y[kw:])
-            total_v[j] = term if fresh else total_v[j] + term
+            term = term * (1.0 / blocks)
+            total_v[j] = total_v[j] + term
             if last:
                 pltpu.make_async_copy(total_v.at[j], out_hbm.at[j], out_sems.at[j]).start()
 
@@ -127,16 +143,16 @@
 
     def first(h, i):
         return pltpu.make_async_remote_copy(
-            g_v.at[h, lax.rem(grp + i, groups)], spread[h].at[grp], s1.at[h, i], r1.at[h, i],
+            g_v.at[h, partner(i)], spread[h].at[grp], s1.at[h, i], r1.at[h, i],
             device_id=group_peer(i), device_id_type=MESH)
 
     def second(h, i):
         return pltpu.make_async_remote_copy(
-            arranged.at[h, lax.rem(grp + i, groups)], out_ref.at[blk, h, grp], s2.at[h, i], r2.at[h, i],
+            arranged.at[h, partner(i)], out_ref.at[blk, h, grp], s2.at[h, i], r2.at[h, i],
             device_id=group_peer(i), device_id_type=MESH)
 
     def third(h, i, k):
-        piece = out_ref.at[blk, h, lax.rem(grp + groups - i, groups)]
+        piece = out_ref.at[blk, h, partner(i)]
         return pltpu.make_async_remote_copy(
             piece, piece, s3.at[h, i, k], r3.at[h, i, k], device_id=block_peer(k), device_id_type=MESH)
 
@@ -159,52 +175,47 @@
         if h > 0:
             finish(h, *chain(h))
 
-        @pl.loop(1, groups)
-        def _(i):
+        for i in pairs:
             first(h, i).start()
 
         spread[h][grp] = g_v[h, grp]
 
+    def forward(h, i):
+        if i:
+            second(h, i).wait_recv()
+        for k in range(1, blocks):
+            third(h, i, k).start()
+
     for h in range(halves):
-        @pl.loop(1, groups)
-        def _(i):
+        for i in pairs:
             first(h, i).wait_recv()
-
-        @pl.loop(1, groups)
-        def _(i):
-            a = lax.rem(grp + i, groups)
+        out_ref[blk, h, grp] = spread[h][source[grp]]
+        for i in pairs:
+            a = partner(i)
             arranged[h, a] = spread[h][source[a]]
             second(h, i).start()
-
-        out_ref[blk, h, grp] = spread[h][source[grp]]
-        for k in range(1, blocks):
-            third(h, 0, k).start()
-
-    for h in range(halves):
-        @pl.loop(1, groups)
-        def _(i):
-            second(h, i).wait_recv()
-            for k in range(1, blocks):
-                third(h, i, k).start()
-
-    accumulate(blk, True, blocks == 1)
+            if h > 0:
+                forward(h - 1, i)
+        forward(h, 0)
+    for i in pairs:
+        forward(halves - 1, i)
+
+    copy_p.wait()
+    accumulate(blk, blocks == 1)
 
     for k in range(1, blocks):
         for h in range(halves):
-            @pl.loop(0, groups)
-            def _(i):
+            for i in [0] + pairs:
                 third(h, i, k).wait_recv()
 
-        accumulate(lax.rem(blk + blocks - k, blocks), False, k == blocks - 1)
+        accumulate(lax.rem(blk + blocks - k, blocks), k == blocks - 1)
 
     for h in range(halves):
-        @pl.loop(0, groups)
-        def _(i):
+        for i in [0] + pairs:
             for k in range(1, blocks):
                 third(h, i, k).wait_send()
 
-        @pl.loop(1, groups)
-        def _(i):
+        for i in pairs:
             first(h, i).wait_send()
             second(h, i).wait_send()
 
@@ -237,7 +248,7 @@
     summed = pl.pallas_call(
         functools.partial(exchange_kernel, groups, blocks),
         out_shape=jax.ShapeDtypeStruct((slots, kw, kw), F32),
-        in_specs=[smem] * 5 + [hbm] * 5,
+        in_specs=[smem] * 5 + [hbm] * 6,
         out_specs=hbm,
         scratch_shapes=[
             pltpu.VMEM((order, order), F32),
@@ -254,7 +265,7 @@
             pltpu.VMEM((slots * kw, kw), BF16),
             pltpu.VMEM((slots, kw, kw), F32),
             pltpu.SMEM((groups,), jnp.int32),
-            pltpu.SemaphoreType.DMA((number + 7,)),
+            pltpu.SemaphoreType.DMA((number + 8,)),
             pltpu.SemaphoreType.DMA((slots,)),
             pltpu.SemaphoreType.DMA((halves, groups)),
             pltpu.SemaphoreType.DMA((halves, groups)),
@@ -267,8 +278,8 @@
             collective_id=0, has_side_effects=True, vmem_limit_bytes=63 * 2**20 + 2**19),
         name="exchange",
     )(assignment, ownership, transfer_momentum, transfer_frequency, momentum_sum,
-      walker_matrix[0, 0], updates[0, 0], update_rows[0, 0], left_table, right_table)
-    return (g4_prior[0] + summed * (1.0 / blocks))[None]
+      walker_matrix[0, 0], updates[0, 0], update_rows[0, 0], left_table, right_table, g4_prior[0])
+    return summed[None]
 
 
 def solution(mesh):

time: 37.7 us -> 36.7 us (0.973)
  other arithmetic: 2.65 us -> 0 us
  local copies, waits for them, and re-layouts: 0 us -> 2.29 us
  Pallas kernels: 34.8 us -> 34.2 us
    broadcast_in_dim x1 -> x0, other arithmetic: 2.65 us -> none  [shards(): return (g4_prior[0] + summed * (1.0 / blocks))[None]]
    unnamed x0 -> x1, local copies, waits for them, and re-layouts: none -> 2.29 us
    pallas_call x1, Pallas kernels: 34.8 us -> 34.2 us  [shards(): pl.pallas_call(functools.partial(exchange_kernel, groups, blocks), out_sh...]
where the time goes in v3:
time: 36.7 us; the launch traced here: 36.5 us
  Pallas kernels  34.2 us (93%)
  local copies, waits for them, and re-layouts  2.29 us (6%)
    pallas_call x1, Pallas kernels, shards(): pl.pallas_call(functools.partial(exchange_kernel, groups, blocks), out_sh...  34.2 us
    unnamed x1, local copies, waits for them, and re-layouts  2.29 us

profile of v3, /device:TPU:0, one launch (start us, length us, event | category | flops | bytes accessed | tf_op | source)
XLA Modules:
  0.0 36.5 jit_solution(7567287496762981216)
XLA Ops:
  0.0 34.2 %exchange.1 = f32[4,256,256]{2,1,0:T(8,128)} custom-call(s32[1,16]{1,0:T(1,128)} %target_ref.1, s32[4]{0:T(128)} %own_ref.1, s32[8]{0:T(128)} %mom_ref.1, s32[8]{0:T(128)} %freq_ref.1, s32[16,16]{1,0:T(8,128)} %sum_ref.1, f32[1024,1024]{1,0:T(8,128)} %bitcast.6, bf16[4,1024,256]{2,1,0:T(8,128)(2,1)} %bitcast.7, s32[4,256]{1,0:T(4,128)} %bitcast.9, ...), custom_call_target="tpu_custom_call" | custom-call | tf_op jit(solution)/shard_map/exchange/pallas_call | solution.py:248
  34.2 2.3 %copy.13 = f32[1,4,256,256]{3,2,1,0:T(8,128)} copy(f32[1,4,256,256]{3,2,1,0:T(8,128)} %bitcast.5) | data formatting | bytes 2097152
